TPU v7x, 32 devices: a whole 2x2x4 slice. The times are simulated.
32 devices in a mesh: dp: 16 (over z, y, x), tensor: 2 (over core).
Axes of the slice: x: 2, y: 2, z: 4, core: 2. Of those that a mesh axis runs over, the one named last changes fastest.
Arguments:
- layer_in: bfloat16 [16384, 1024], P(('dp', 'tensor')), may hold values from -6 to 6
- w_qkv: bfloat16 [3, 1024, 1024], P(None, 'dp', 'tensor'), may hold values from -1 to 1
- b_qv: bfloat16 [2, 16, 64], P(None, 'tensor', 'dp'), may hold values from -3 to 3
- w_proj: bfloat16 [1024, 1024], P('tensor', 'dp'), may hold values from -0.5 to 0.5
- w_ff1: bfloat16 [1024, 4096], P('dp', 'tensor'), may hold values from -0.1875 to 0.1875
- b_ff1: bfloat16 [64, 64], P('tensor', 'dp'), may hold values from -3 to 3
- w_ff2: bfloat16 [4096, 1024], P('tensor', 'dp'), may hold values from -0.09375 to 0.09375
- norm_gains: float32 [2, 1024], P(None, ('dp', 'tensor')), may hold values from 0.5 to 1.5
- add_biases: float32 [4, 1024], P(None, ('dp', 'tensor')), may hold values from -3 to 3
- cotangent: bfloat16 [16384, 1024], P(('dp', 'tensor')), may hold values from -6 to 6
Outputs:
- layer_out: bfloat16 [16384, 1024], P(('dp', 'tensor'))
- grad_in: float32 [16384, 1024], P(('dp', 'tensor'))
- grad_w_qkv: float32 [3, 1024, 1024], P(None, 'dp', 'tensor')
- grad_b_qv: float32 [2, 16, 64], P(None, 'tensor', 'dp')
- grad_w_proj: float32 [1024, 1024], P('tensor', 'dp')
- grad_w_ff1: float32 [1024, 4096], P('dp', 'tensor')
- grad_b_ff1: float32 [64, 64], P('tensor', 'dp')
- grad_w_ff2: float32 [4096, 1024], P('tensor', 'dp')
- grad_gains: float32 [2, 1024], P(None, ('dp', 'tensor'))
- grad_biases: float32 [4, 1024], P(None, ('dp', 'tensor'))
All inputs are finite; a program needn't handle non-finite values.
Results may differ from a plain program's by a relative error of at most 0.015.
Values may be sent and summed in bfloat16 or wider, within the bound.
A program may use at most 192 MiB of HBM per device.

v0:
```python
import jax
import jax.numpy as jnp
from jax import lax
from jax.sharding import PartitionSpec as P

H = 16
HD = 64
SEQ_LEN = 1024


epsilon = 1e-05
gelu_scale = 0.7978845608028654


def gelu_tanh(inputs):
    return (
        0.5 * inputs * (1.0 + jnp.tanh(gelu_scale * (inputs + 0.044715 * inputs * inputs * inputs)))
    )


def norm_rows(values, gain_row, shift_row):
    center = values - jnp.mean(values, axis=-1, keepdims=True)
    spread = jnp.mean(center * center, axis=-1, keepdims=True)
    inverse = lax.rsqrt(spread + epsilon)
    normed = center * inverse
    return (normed * gain_row + shift_row, normed, inverse)


def norm_back(grad_rows, normed, inverse, gain_row):
    scaled = grad_rows * gain_row
    return inverse * (
        scaled
        - jnp.mean(scaled, axis=-1, keepdims=True)
        - normed * jnp.mean(scaled * normed, axis=-1, keepdims=True)
    )


def contract_rows(left, right):
    return lax.dot_general(
        left, right, (((0,), (0,)), ((), ())), preferred_element_type=jnp.float32
    )


def times_transposed(left, right):
    return lax.dot_general(
        left, right, (((1,), (1,)), ((), ())), preferred_element_type=jnp.float32
    )


def gather_rows(piece):
    return lax.all_gather(piece, "tensor", axis=0, tiled=True)


def sum_rows(term_fn, row_count):
    return lax.psum_scatter(
        term_fn(jnp.int32(0), row_count * lax.axis_size("tensor")).astype(jnp.bfloat16),
        "tensor",
        scatter_dimension=0,
        tiled=True,
    ).astype(jnp.float32)


def fetch_attention(w_qkv, b_qv, w_proj):
    return (
        lax.all_gather(w_qkv, "dp", axis=1, tiled=True),
        lax.all_gather(b_qv, "dp", axis=2, tiled=True),
        lax.all_gather(w_proj, "dp", axis=1, tiled=True),
    )


def fetch_mlp(w_ff1, b_ff1, w_ff2):
    return (
        lax.all_gather(w_ff1, "dp", axis=0, tiled=True),
        lax.all_gather(b_ff1, "dp", axis=1, tiled=True),
        lax.all_gather(w_ff2, "dp", axis=1, tiled=True),
    )


def head_slopes(heads_dev):
    head_order = (
        lax.axis_index("tensor") * heads_dev + jnp.arange(heads_dev, dtype=jnp.int32) + 1
    ).astype(jnp.float32)
    return 2.0 ** (-8.0 * head_order / H)


def block_scores(queries, keys_all, slopes, q_start):
    block_len = queries.shape[1]
    key_count = keys_all.shape[1]
    scores = jnp.einsum(
        "sqhd,skhd->shqk", queries, keys_all, preferred_element_type=jnp.float32
    ) * HD ** (-0.5)
    query_pos = q_start + jnp.arange(block_len, dtype=jnp.int32)
    key_pos = jnp.arange(key_count, dtype=jnp.int32)
    offsets = (key_pos[None, :] - query_pos[:, None]).astype(jnp.float32)
    scores = scores + slopes[:, None, None] * offsets
    return jnp.where(key_pos[None, :] <= query_pos[:, None], scores, -1e30)


def attend(queries, keys_all, values_all, slopes):
    block_len = min(512, SEQ_LEN)
    outputs = []
    log_sums = []
    for q_start in range(0, SEQ_LEN, block_len):
        q_end = q_start + block_len
        scores = block_scores(queries[:, q_start:q_end], keys_all[:, :q_end], slopes, q_start)
        row_peak = jnp.max(scores, axis=-1, keepdims=True)
        expweights = jnp.exp(scores - row_peak)
        row_total = jnp.sum(expweights, axis=-1, keepdims=True)
        attn_probs = (expweights / row_total).astype(jnp.bfloat16)
        block_out = jnp.einsum(
            "shqk,skhd->sqhd", attn_probs, values_all[:, :q_end], preferred_element_type=jnp.float32
        )
        outputs.append(block_out.astype(jnp.bfloat16))
        log_sums.append((row_peak + jnp.log(row_total))[..., 0])
    return (jnp.concatenate(outputs, axis=1), jnp.concatenate(log_sums, axis=2))


def attend_back(queries, keys_all, values_all, grad_out, log_sums, slopes):
    block_len = min(512, SEQ_LEN)
    grad_keys = jnp.zeros(keys_all.shape, jnp.float32)
    grad_values = jnp.zeros(values_all.shape, jnp.float32)
    grad_queries = []
    for q_start in range(0, SEQ_LEN, block_len):
        q_end = q_start + block_len
        query_part = queries[:, q_start:q_end]
        grad_part = grad_out[:, q_start:q_end]
        scores = block_scores(query_part, keys_all[:, :q_end], slopes, q_start)
        attn_probs = jnp.exp(scores - log_sums[:, :, q_start:q_end, None])
        probs_low = attn_probs.astype(jnp.bfloat16)
        grad_probs = jnp.einsum(
            "sqhd,skhd->shqk", grad_part, values_all[:, :q_end], preferred_element_type=jnp.float32
        )
        row_inner = jnp.sum(grad_probs * attn_probs, axis=-1, keepdims=True)
        grad_scores = (attn_probs * (grad_probs - row_inner)).astype(jnp.bfloat16)
        grad_queries.append(
            jnp.einsum(
                "shqk,skhd->sqhd",
                grad_scores,
                keys_all[:, :q_end],
                preferred_element_type=jnp.float32,
            )
            * HD ** (-0.5)
        )
        key_term = jnp.einsum(
            "shqk,sqhd->skhd", grad_scores, query_part, preferred_element_type=jnp.float32
        ) * HD ** (-0.5)
        grad_keys = grad_keys.at[:, :q_end].add(key_term)
        value_term = jnp.einsum(
            "shqk,sqhd->skhd", probs_low, grad_part, preferred_element_type=jnp.float32
        )
        grad_values = grad_values.at[:, :q_end].add(value_term)
    return (jnp.concatenate(grad_queries, axis=1), grad_keys, grad_values)


def on_device(
    layer_in, w_qkv, b_qv, w_proj, w_ff1, b_ff1, w_ff2, norm_gains, add_biases, cotangent
):
    gain_all, shift_all = (
        lax.all_gather(norm_gains, ("dp", "tensor"), axis=1, tiled=True),
        lax.all_gather(add_biases, ("dp", "tensor"), axis=1, tiled=True),
    )
    local_rows = layer_in.shape[0]
    resid = layer_in.astype(jnp.float32)
    act_one, normed_one, inverse_one = norm_rows(resid, gain_all[0], shift_all[0])
    full_one = gather_rows(act_one.astype(jnp.bfloat16))
    rows_all = full_one.shape[0]
    seq_here = rows_all // SEQ_LEN
    qkv_w, qv_bias, proj_w = fetch_attention(w_qkv, b_qv, w_proj)
    heads_dev = qv_bias.shape[1]
    width_dev = qkv_w.shape[2]
    bias_flat = qv_bias.reshape(2, width_dev).astype(jnp.float32)
    mixed = jnp.einsum("rd,cde->cre", full_one, qkv_w, preferred_element_type=jnp.float32)
    head_shape = (seq_here, SEQ_LEN, heads_dev, HD)
    queries = (mixed[0] + bias_flat[0]).astype(jnp.bfloat16).reshape(head_shape)
    keys_all = mixed[1].astype(jnp.bfloat16).reshape(head_shape)
    values_all = (mixed[2] + bias_flat[1]).astype(jnp.bfloat16).reshape(head_shape)
    slopes = head_slopes(heads_dev)
    attended, log_sums = attend(queries, keys_all, values_all, slopes)
    attn_flat = attended.reshape(rows_all, width_dev)

    def project(start, count):
        return jnp.dot(attn_flat, proj_w, preferred_element_type=jnp.float32)

    middle = resid + sum_rows(project, local_rows) + shift_all[1]
    act_two, normed_two, inverse_two = norm_rows(middle, gain_all[1], shift_all[2])
    act_low = act_two.astype(jnp.bfloat16)
    up_w, up_bias, down_w = fetch_mlp(w_ff1, b_ff1, w_ff2)
    grad_three = cotangent.astype(jnp.float32)
    full_two = gather_rows(act_low)
    hidden_pre = jnp.dot(full_two, up_w, preferred_element_type=jnp.float32) + up_bias.reshape(
        -1
    ).astype(jnp.float32)
    hidden = gelu_tanh(hidden_pre).astype(jnp.bfloat16)

    def lower(start, count):
        return jnp.dot(hidden, down_w, preferred_element_type=jnp.float32)

    layer_out = (middle + sum_rows(lower, local_rows) + shift_all[3]).astype(jnp.bfloat16)
    full_cot = gather_rows(cotangent)
    up_w, up_bias, down_w = fetch_mlp(w_ff1, b_ff1, w_ff2)
    grad_hidden = times_transposed(full_cot, down_w)
    grad_down = contract_rows(hidden, full_cot)
    unused_value, gelu_pull = jax.vjp(gelu_tanh, hidden_pre)
    grad_pre = gelu_pull(grad_hidden)[0].astype(jnp.bfloat16)
    grad_up_bias = jnp.sum(grad_pre, axis=0, dtype=jnp.float32).reshape(up_bias.shape)
    grad_up = contract_rows(full_two, grad_pre)

    def back_up(start, count):
        return times_transposed(grad_pre, up_w)

    grad_act_two = sum_rows(back_up, local_rows)
    grad_up, grad_up_bias, grad_down = (
        lax.psum_scatter(grad_up, "dp", scatter_dimension=0, tiled=True),
        lax.psum_scatter(grad_up_bias, "dp", scatter_dimension=1, tiled=True),
        lax.psum_scatter(grad_down, "dp", scatter_dimension=1, tiled=True),
    )
    grad_mid = grad_three + norm_back(grad_act_two, normed_two, inverse_two, gain_all[1])
    grad_gain_two = jnp.sum(grad_act_two * normed_two, axis=0)
    grad_shift_two = jnp.sum(grad_act_two, axis=0)
    grad_out_bias = jnp.sum(grad_three, axis=0)
    grad_proj_bias = jnp.sum(grad_mid, axis=0)
    full_mid = gather_rows(grad_mid.astype(jnp.bfloat16))
    qkv_w, qv_bias, proj_w = fetch_attention(w_qkv, b_qv, w_proj)
    grad_attn = times_transposed(full_mid, proj_w).astype(jnp.bfloat16).reshape(head_shape)
    grad_proj = contract_rows(attn_flat, full_mid)
    grad_q, grad_k, grad_v = attend_back(queries, keys_all, values_all, grad_attn, log_sums, slopes)
    grad_qkv = jnp.stack(
        [
            part.reshape(rows_all, width_dev).astype(jnp.bfloat16)
            for part in (grad_q, grad_k, grad_v)
        ]
    )
    grad_qkv_w = jnp.einsum("rd,cre->cde", full_one, grad_qkv, preferred_element_type=jnp.float32)
    grad_qv_bias = jnp.sum(grad_qkv[0::2], axis=1, dtype=jnp.float32).reshape(2, heads_dev, HD)
    grad_qkv_w, grad_qv_bias, grad_proj = (
        lax.psum_scatter(grad_qkv_w, "dp", scatter_dimension=1, tiled=True),
        lax.psum_scatter(grad_qv_bias, "dp", scatter_dimension=2, tiled=True),
        lax.psum_scatter(grad_proj, "dp", scatter_dimension=1, tiled=True),
    )

    def back_in(start, count):
        return jnp.einsum("cre,cde->rd", grad_qkv, qkv_w, preferred_element_type=jnp.float32)

    grad_act_one = sum_rows(back_in, local_rows)
    grad_in = grad_mid + norm_back(grad_act_one, normed_one, inverse_one, gain_all[0])
    grad_gain_one = jnp.sum(grad_act_one * normed_one, axis=0)
    grad_shift_one = jnp.sum(grad_act_one, axis=0)
    gain_terms = jnp.stack([grad_gain_one, grad_gain_two])
    bias_terms = jnp.stack([grad_shift_one, grad_proj_bias, grad_shift_two, grad_out_bias])
    grad_gains, grad_biases = (
        lax.psum_scatter(gain_terms, ("dp", "tensor"), scatter_dimension=1, tiled=True),
        lax.psum_scatter(bias_terms, ("dp", "tensor"), scatter_dimension=1, tiled=True),
    )
    return (
        layer_out,
        grad_in,
        grad_qkv_w,
        grad_qv_bias,
        grad_proj,
        grad_up,
        grad_up_bias,
        grad_down,
        grad_gains,
        grad_biases,
    )


def solution(mesh):
    placed = (
        P(("dp", "tensor"), None),
        P(None, "dp", "tensor"),
        P(None, "tensor", "dp"),
        P("tensor", "dp"),
        P("dp", "tensor"),
        P("tensor", "dp"),
        P("tensor", "dp"),
        P(None, ("dp", "tensor")),
        P(None, ("dp", "tensor")),
        P(("dp", "tensor"), None),
    )
    return jax.shard_map(
        on_device,
        mesh=mesh,
        in_specs=placed,
        out_specs=(
            P(("dp", "tensor"), None),
            P(("dp", "tensor"), None),
            P(None, "dp", "tensor"),
            P(None, "tensor", "dp"),
            P("tensor", "dp"),
            P("dp", "tensor"),
            P("tensor", "dp"),
            P("tensor", "dp"),
            P(None, ("dp", "tensor")),
            P(None, ("dp", "tensor")),
        ),
        check_vma=False,
    )
```

profile of v0, /device:TPU:0, one launch (start us, length us, event | category | flops | bytes accessed | tf_op | source)
XLA Modules:
  0.0 1548.0 jit_solution(14423853497930877390)
XLA Ops:
  10.3 43.6 %all-gather = f32[32,32,2]{1,2,0:T(2,128)S(1)} all-gather(f32[1,32,2]{1,2,0:T(2,128)} %bitcast.207), channel_id=1, replica_groups=mesh['dp'=16,'tensor'=2] {'dp','tensor'}, dimensions={0}, use_global_device_ids=true | all-gather | bytes 8448 | tf_op jit(solution)/shard_map/all_gather | solution.py:159
  54.1 37.1 %all-gather.1 = f32[32,32,4]{1,2,0:T(4,128)S(1)} all-gather(f32[1,32,4]{1,2,0:T(4,128)} %bitcast.206), channel_id=1, replica_groups=mesh['dp'=16,'tensor'=2] {'dp','tensor'}, dimensions={0}, use_global_device_ids=true | all-gather | bytes 16896 | tf_op jit(solution)/shard_map/all_gather | solution.py:160
  98.4 37.7 %all_gather.44 = bf16[2,8,64]{1,0,2:T(2,128)(2,1)S(1)} all-gather(bf16[2,8,4]{1,0,2:T(2,128)(2,1)S(1)} %copy.51), channel_id=1, replica_groups=mesh['dp'=16,'tensor'=2] {'dp'}, dimensions={2}, use_global_device_ids=true | all-gather | bytes 2176 | tf_op jit(solution)/shard_map/all_gather | solution.py:66
  136.2 37.7 %all-gather.14.cloned.1.call-done = bf16[3,1024,512]{2,1,0:T(8,128)(2,1)} async-done(((bf16[3,64,512]{2,1,0:T(8,128)(2,1)}), bf16[3,1024,512]{2,1,0:T(8,128)(2,1)}) %all-gather.14.cloned.1.call-update) | async-done | bytes 3145744 | tf_op jit(solution)/shard_map/all_gather | solution.py:65
  207.7 22.7 %all-gather.16.cloned.1.call-done = bf16[512,1024]{0,1:T(8,128)(2,1)} async-done(((bf16[512,64]{0,1:T(8,128)(2,1)}), bf16[512,1024]{0,1:T(8,128)(2,1)}) %all-gather.16.cloned.1.call-update) | async-done | bytes 1048592 | tf_op jit(solution)/shard_map/all_gather | solution.py:67
  249.9 41.4 %all-gather.2 = bf16[16,4,32]{2,1,0:T(4,128)(2,1)S(1)} all-gather(bf16[1,4,32]{2,1,0:T(4,128)(2,1)S(1)} %bitcast.208), channel_id=1, replica_groups=mesh['dp'=16,'tensor'=2] {'dp'}, dimensions={0}, use_global_device_ids=true | all-gather | bytes 4352 | tf_op jit(solution)/shard_map/all_gather | solution.py:74
  291.4 31.1 %all-gather.20.cloned.1.call-done = bf16[1024,2048]{1,0:T(8,128)(2,1)} async-done(((bf16[64,2048]{1,0:T(8,128)(2,1)}), bf16[1024,2048]{1,0:T(8,128)(2,1)}) %all-gather.20.cloned.1.call-update) | async-done | bytes 4194320 | tf_op jit(solution)/shard_map/all_gather | solution.py:73
  322.4 11.2 all-gather.18.cloned.1.call-done
  333.6 10.9 fusion.75
  346.9 79.6 %all-gather.22.cloned.1.call-done = bf16[2048,1024]{0,1:T(8,128)(2,1)} async-done(((bf16[2048,64]{0,1:T(8,128)(2,1)}), bf16[2048,1024]{0,1:T(8,128)(2,1)}) %all-gather.22.cloned.1.call-update) | async-done | bytes 4194320 | tf_op jit(solution)/shard_map/all_gather | solution.py:75
  426.5 14.4 convert_reduce_fusion
  448.8 11.3 convolution_convert_fusion.1
  476.6 11.9 all-gather.26.cloned.1.call-done
  506.0 11.3 multiply_reduce_fusion
  528.0 11.8 multiply_convert_fusion
  554.8 11.0 reduce-scatter.21.cloned.1.call-done
  578.4 9.4 copy.64
  593.5 12.1 fusion.66
  621.6 78.1 %all-reduce.5 = (f32[2,8,64]{1,0,2:T(2,128)S(1)}, f32[32,64]{1,0:T(8,128)S(1)}) all-reduce(f32[2,8,64]{1,0,2:T(2,128)S(1)} %copy.65, f32[32,64]{1,0:T(8,128)S(1)} %reshape.546), channel_id=7, replica_groups=mesh['dp'=16,'tensor'=2] {'dp'}, use_global_device_ids=true, to_apply=%region_20.21.clone | all-reduce | flops 3072 | bytes 24576
  708.0 132.1 %reduce-scatter.31.cloned.1.call-done = f32[32,4]{1,0:T(8,128)} async-done(((f32[1024,4]{1,0:T(8,128)}), f32[32,4]{1,0:T(8,128)}) %reduce-scatter.31.cloned.1.call-update) | async-done | bytes 528
  841.4 256.1 %all-reduce.8.cloned.1.call-done = f32[3,1024,512]{2,0,1:T(4,128)} async-done(((f32[3,1024,512]{2,0,1:T(4,128)}), f32[3,1024,512]{2,0,1:T(4,128)}) %all-reduce.8.cloned.1.call-update) | async-done | bytes 6291472
  1099.5 81.4 %reduce-scatter.23.cloned.1.call-done = f32[512,64]{0,1:T(8,128)} async-done(((f32[512,1024]{0,1:T(8,128)}), f32[512,64]{0,1:T(8,128)}) %reduce-scatter.23.cloned.1.call-update) | async-done | bytes 131088 | tf_op jit(solution)/shard_map/reduce_scatter | solution.py:238
  1180.8 177.1 %reduce-scatter.27.cloned.1.call-done = f32[2048,64]{0,1:T(8,128)} async-done(((f32[2048,1024]{0,1:T(8,128)}), f32[2048,64]{0,1:T(8,128)}) %reduce-scatter.27.cloned.1.call-update) | async-done | bytes 524304 | tf_op jit(solution)/shard_map/reduce_scatter | solution.py:215
  1357.9 183.0 %reduce-scatter.25.cloned.1.call-done = f32[64,2048]{1,0:T(8,128)} async-done(((f32[1024,2048]{1,0:T(8,128)}), f32[64,2048]{1,0:T(8,128)}) %reduce-scatter.25.cloned.1.call-update) | async-done | bytes 524304 | tf_op jit(solution)/shard_map/reduce_scatter | solution.py:213
  (197 shorter events, 178.0 us)
Async XLA Ops:
  7.2 129.1 %all-gather.12.cloned.1.call-start = ((), (), s32[]{:S(2)}) async-start(), calls=%async_computation.9 | async-start | bytes 3145728 | tf_op jit(solution)/shard_map/all_gather | solution.py:51
  8.7 89.7 %copy-start.22 = (f32[512]{0:T(512)}, f32[512]{0:T(512)S(1)}, u32[]{:S(2)}) copy-start(f32[512]{0:T(512)S(1)} %broadcast_multiply_fusion.5) | copy-start | bytes 6148
  8.7 89.7 %copy-start.26 = (bf16[2,8,4]{1,2,0:T(4,128)(2,1)S(1)}, bf16[2,8,4]{1,2,0:T(4,128)(2,1)}, u32[]{:S(2)}) copy-start(bf16[2,8,4]{1,2,0:T(4,128)(2,1)} %param.24) | copy-start | bytes 388
  10.3 169.8 %copy-start.24 = (f32[512]{0:T(512)}, f32[512]{0:T(512)S(1)}, u32[]{:S(2)}) copy-start(f32[512]{0:T(512)S(1)} %add_rsqrt_fusion.1) | copy-start | bytes 6148
  54.0 126.1 %copy-start.20 = (f32[1,1024]{1,0:T(1,128)}, f32[1,1024]{1,0:T(1,128)S(1)}, u32[]{:S(2)}) copy-start(f32[1,1024]{1,0:T(1,128)S(1)} %get-tuple-element.128) | copy-start | bytes 12292
  93.9 80.0 %all-gather.14.cloned.1.call-start = ((), (), s32[]{:S(2)}) async-start(), calls=%async_computation.10 | async-start | bytes 3342336 | tf_op jit(solution)/shard_map/all_gather | solution.py:65
  94.7 135.8 %all-gather.16.cloned.1.call-start = ((), (), s32[]{:S(2)}) async-start(), calls=%async_computation.11 | async-start | bytes 1114112 | tf_op jit(solution)/shard_map/all_gather | solution.py:67
  95.4 147.8 %reduce-scatter.15.cloned.1.call-start = ((), (), s32[]{:S(2)}) async-start(), calls=%async_computation.12 | async-start | bytes 3145728 | tf_op jit(solution)/shard_map/reduce_scatter | solution.py:55
  207.7 26.7 %copy-start.17 = (bf16[1,1024,8,64]{1,3,2,0:T(8,128)(2,1)}, bf16[1,1024,8,64]{1,3,2,0:T(8,128)(2,1)S(1)}, u32[]{:S(2)}) copy-start(bf16[1,1024,8,64]{1,3,2,0:T(8,128)(2,1)S(1)} %pad_maximum_fusion.1) | copy-start | bytes 3145732
  234.4 88.0 %all-gather.20.cloned.1.call-start = ((), (), s32[]{:S(2)}) async-start(), calls=%async_computation.14 | async-start | bytes 4456448 | tf_op jit(solution)/shard_map/all_gather | solution.py:73
  235.0 98.6 %all-gather.18.cloned.1.call-start = ((), (), s32[]{:S(2)}) async-start(), calls=%async_computation.13 | async-start | bytes 3145728 | tf_op jit(solution)/shard_map/all_gather | solution.py:51
  248.3 98.6 %all-gather.24.cloned.1.call-start = ((), (), s32[]{:S(2)}) async-start(), calls=%async_computation.17 | async-start | bytes 3145728 | tf_op jit(solution)/shard_map/all_gather | solution.py:51
  249.1 177.5 %all-gather.22.cloned.1.call-start = ((), (), s32[]{:S(2)}) async-start(), calls=%async_computation.15 | async-start | bytes 4456448 | tf_op jit(solution)/shard_map/all_gather | solution.py:75
  249.8 210.4 %reduce-scatter.19.cloned.1.call-start = ((), (), s32[]{:S(2)}) async-start(), calls=%async_computation.18 | async-start | bytes 3145728 | tf_op jit(solution)/shard_map/reduce_scatter | solution.py:55
  448.6 21.7 %reduce-scatter.17.cloned.1.call-start = ((), (), s32[]{:S(2)}) async-start(), calls=%async_computation.16 | async-start | bytes 3145728 | tf_op jit(solution)/shard_map/reduce_scatter | solution.py:55
  460.2 28.3 %all-gather.26.cloned.1.call-start = ((), (), s32[]{:S(2)}) async-start(), calls=%async_computation.19 | async-start | bytes 3145728 | tf_op jit(solution)/shard_map/all_gather | solution.py:51
  476.5 89.4 %reduce-scatter.21.cloned.1.call-start = ((), (), s32[]{:S(2)}) async-start(), calls=%async_computation.20 | async-start | bytes 3145728 | tf_op jit(solution)/shard_map/reduce_scatter | solution.py:55
  554.8 151.8 %reduce-scatter.29.cloned.1.call-start = ((), (), s32[]{:S(2)}) async-start(), calls=%async_computation.24 | async-start | bytes 540672
  569.2 270.9 %reduce-scatter.31.cloned.1.call-start = ((), (), s32[]{:S(2)}) async-start(), calls=%async_computation.25 | async-start | bytes 540672
  570.3 527.2 %all-reduce.8.cloned.1.call-start = ((), (), s32[]{:S(2)}) async-start(), calls=%async_computation.26 | async-start | bytes 16777216
  587.8 593.0 %reduce-scatter.23.cloned.1.call-start = ((), (), s32[]{:S(2)}) async-start(), calls=%async_computation.21 | async-start | bytes 2228224 | tf_op jit(solution)/shard_map/reduce_scatter | solution.py:238
  593.3 764.7 %reduce-scatter.27.cloned.1.call-start = ((), (), s32[]{:S(2)}) async-start(), calls=%async_computation.23 | async-start | bytes 8912896 | tf_op jit(solution)/shard_map/reduce_scatter | solution.py:215
  605.6 935.4 %reduce-scatter.25.cloned.1.call-start = ((), (), s32[]{:S(2)}) async-start(), calls=%async_computation.22 | async-start | bytes 8912896 | tf_op jit(solution)/shard_map/reduce_scatter | solution.py:213
  618.7 82.3 %copy-start.6 = (f32[512,1024]{1,0:T(8,128)S(1)}, f32[512,1024]{1,0:T(8,128)}, u32[]{:S(2)}) copy-start(f32[512,1024]{1,0:T(8,128)} %copy-done.5) | copy-start | bytes 6291460
  (28 other events, 216.6 us)
Sparse Core Ops, SparseCore 0:
  94.0 7.9 all-gather.11
  104.8 69.0 all-gather.13
  176.7 53.7 all-gather.15
  234.5 8.5 reduce-scatter.14
  245.8 76.6 all-gather.19
  324.4 9.1 all-gather.17
  335.2 11.7 all-gather.23
  349.7 76.7 all-gather.21
  448.7 8.3 reduce-scatter.18
  460.3 9.9 reduce-scatter.16
  476.6 11.8 all-gather.25
  554.9 10.8 reduce-scatter.20
  569.3 137.2 reduce-scatter.28
  708.7 131.2 reduce-scatter.30
  845.9 251.5 all-reduce.7
  1100.2 80.6 reduce-scatter.22
  1183.6 174.2 reduce-scatter.26
  1360.6 180.2 reduce-scatter.24
where the time goes:
time: 1550 us
  waiting for transfers between devices  1060 us (68%)
  blocking collectives  238 us (15%)
  matrix products  145 us (9%)
  other arithmetic  49 us (3%)
  local copies, waits for them, and re-layouts  40 us (3%)
  between operations  16.4 us (1%)
    unnamed x21, waiting for transfers between devices  394 us
    reduce_scatter x1, waiting for transfers between devices, on_device(): lax.psum_scatter(grad_up, 'dp', scatter_dimension=0, tiled=True)  183 us
    reduce_scatter x1, waiting for transfers between devices, on_device(): lax.psum_scatter(grad_down, 'dp', scatter_dimension=1, tiled=True)  177 us
    reduce_scatter x1, waiting for transfers between devices, on_device(): lax.psum_scatter(grad_proj, 'dp', scatter_dimension=1, tiled=True)  81.4 us
    all_gather x1, waiting for transfers between devices, fetch_mlp(): lax.all_gather(w_ff2, 'dp', axis=1, tiled=True)  79.6 us
    unnamed x1, blocking collectives  78.1 us
    all_gather x1, blocking collectives, on_device(): lax.all_gather(norm_gains, ('dp', 'tensor'), axis=1, tiled=True)  43.6 us
    all_gather x1, blocking collectives, fetch_mlp(): lax.all_gather(b_ff1, 'dp', axis=1, tiled=True)  41.4 us
  transfers between devices with their start and end apart: 18, of which 16 were waited for; matrix products, arithmetic and copies ran while one was open for 7% of the time, Pallas kernels for 0%

commit v1 on v0

v1 whole, which is shorter than its diff:
```python
import functools
import math
import jax
import jax.numpy as jnp
from jax import lax
from jax.experimental import pallas as pl
from jax.experimental.pallas import tpu as pltpu
from jax.sharding import PartitionSpec as P

MESH = pl.DeviceIdType.MESH
ANY = pl.BlockSpec(memory_space=pl.ANY)
VM = pl.BlockSpec(memory_space=pltpu.VMEM)


def bits_of(index, count):
    return [lax.rem(index // (1 << b), 2) for b in range(count)]


def partner_of(index, mine, b):
    return index + (1 - 2 * mine[b]) * (1 << b)


def halving_orders(count):
    return [[(start + i) % count for i in range(count)] for start in range(3)]


def enter(index, mine, count, other):
    barrier = pltpu.get_barrier_semaphore()
    for b in range(count):
        pl.semaphore_signal(barrier, inc=1, device_id={"dp": partner_of(index, mine, b)}, device_id_type=MESH)
    pl.semaphore_signal(barrier, inc=1, device_id={"tensor": other}, device_id_type=MESH)
    pl.semaphore_wait(barrier, count + 1)


def block_index(mine, held, count):
    return tuple(slice(None) if b in held else mine[b] for b in reversed(range(count)))


PATTERN = (0, 1, 0, 1, 0, 1, 0, 2)

def gather_kernel(count, chunks, qkv, proj, up, down, small, x, cot,
                  qkv_o, proj_o, up_o, down_o, small_o, x_o, cot_o,
                  send, recv, own_sem, pair_send, pair_recv):
    me = lax.axis_index("dp")
    t = lax.axis_index("tensor")
    other = 1 - t
    mine = bits_of(me, count)
    orders = [o[::-1] for o in halving_orders(count)]
    full = block_index(mine, (), count)

    def views(c):
        name, lead, lo, size = chunks[c]
        src = {"qkv": qkv, "proj": proj, "up": up, "down": down, "small": small}[name]
        dst = {"qkv": qkv_o, "proj": proj_o, "up": up_o, "down": down_o, "small": small_o}[name]
        if name == "small":
            return src, dst.at[t], (slice(None), slice(None))
        if lead is not None:
            src, dst = src.at[lead], dst.at[lead]
        return src.at[:, pl.ds(lo, size)], dst, (slice(None), pl.ds(lo, size))

    enter(me, mine, count, other)
    local_rows = x.shape[0]
    rows = pl.ds(t * local_rows, local_rows)
    pairs = []
    for i, (s, d) in enumerate(((x, x_o), (cot, cot_o))):
        cp = pltpu.make_async_remote_copy(s, d.at[rows], pair_send.at[i], pair_recv.at[i], device_id={"tensor": other}, device_id_type=MESH)
        cp.start()
        own = pltpu.make_async_copy(s, d.at[rows], own_sem.at[len(chunks) + i])
        own.start()
        pairs += [cp, own]
    owns = []
    for c in range(len(chunks)):
        src, dst, tail = views(c)
        cp = pltpu.make_async_copy(src, dst.at[(*full, *tail)], own_sem.at[c])
        cp.start()
        owns.append(cp)
    sent = {}
    steps = sorted(((c, s) for c in range(len(chunks)) for s in range(count)), key=lambda cs: (cs[0] + 2 * cs[1], cs[0]))
    for c, s in steps:
        order = orders[0] if chunks[c][0] == "small" else orders[PATTERN[c % 8]]
        src, dst, tail = views(c)
        if s == 1:
            owns[c].wait()
        if s > 0:
            sent[c, s - 1].wait_recv()
        at = (*block_index(mine, order[:s], count), *tail)
        cp = pltpu.make_async_remote_copy(src if s == 0 else dst.at[at], dst.at[at], send.at[c * count + s], recv.at[c * count + s],
                                          device_id={"dp": partner_of(me, mine, order[s])}, device_id_type=MESH)
        cp.start()
        sent[c, s] = cp
    for c in range(len(chunks)):
        sent[c, count - 1].wait_recv()
    last = pltpu.make_async_remote_copy(small_o.at[t], small_o.at[t], pair_send.at[2], pair_recv.at[2], device_id={"tensor": other}, device_id_type=MESH)
    last.start()
    for cp in sent.values():
        cp.wait_send()
    for cp in pairs:
        cp.wait()
    last.wait()


def gather_all(qkv, proj, up, down, small, x, cot, n, width=512):
    count = n.bit_length() - 1
    two = (2,) * count
    chunks = [("small", None, 0, 0)]
    for c in range(3):
        chunks += [("qkv", c, lo, width) for lo in range(0, qkv.shape[2], width)]
    for name, a in (("proj", proj), ("up", up), ("down", down)):
        chunks += [(name, None, lo, width) for lo in range(0, a.shape[1], width)]
    sd = lambda s, d: jax.ShapeDtypeStruct(s, d)
    outs = (sd((3, *two, *qkv.shape[1:]), jnp.bfloat16), sd((*two, *proj.shape), jnp.bfloat16), sd((*two, *up.shape), jnp.bfloat16),
            sd((*two, *down.shape), jnp.bfloat16), sd((2, *two, *small.shape), jnp.float32),
            sd((2 * x.shape[0], x.shape[1]), x.dtype), sd((2 * x.shape[0], x.shape[1]), x.dtype))
    k = len(chunks)
    res = pl.pallas_call(
        functools.partial(gather_kernel, count, chunks), out_shape=outs,
        in_specs=[VM] * 7, out_specs=[ANY] * 7,
        scratch_shapes=[pltpu.SemaphoreType.DMA((k * count,)), pltpu.SemaphoreType.DMA((k * count,)), pltpu.SemaphoreType.DMA((k + 2,)),
                        pltpu.SemaphoreType.DMA((3,)), pltpu.SemaphoreType.DMA((3,))],
        compiler_params=pltpu.CompilerParams(collective_id=0, has_side_effects=True), name="gather_all",
    )(qkv, proj, up, down, small, x, cot)
    return res


def scatter_kernel(count, chunks, width, qkv, proj, up, down, small, qkv_o, proj_o, up_o, down_o, small_o, pair_o,
                   acc, sacc, load_sem, send, recv, pair_sem, *landing):
    land, sland = landing[:count], landing[count:]
    me = lax.axis_index("dp")
    t = lax.axis_index("tensor")
    other = 1 - t
    mine = bits_of(me, count)
    orders = halving_orders(count)
    enter(me, mine, count, other)

    def src_view(c):
        name, lead, lo, size = chunks[c]
        if name == "small":
            return small, (slice(None), slice(None))
        ref = {"qkv": qkv, "proj": proj, "up": up, "down": down}[name]
        if lead is not None:
            ref = ref.at[lead]
        return ref, (slice(None), pl.ds(lo, size))

    def order_of(c):
        return orders[0] if chunks[c][0] == "small" else orders[PATTERN[c % 8]]

    def bufs(c):
        if chunks[c][0] == "small":
            return sacc, sland
        return acc.at[c - 1], tuple(r.at[c - 1] for r in land)

    def pick(c, s, flip):
        order = order_of(c)
        out = []
        for b in reversed(range(count)):
            if s > 0 and b == order[0]:
                continue
            if b == order[s]:
                out.append(1 - mine[b] if flip else mine[b])
            elif b in order[:s]:
                out.append(mine[b])
            else:
                out.append(slice(None))
        return tuple(out)

    loads = []
    for c in range(len(chunks)):
        ref, tail = src_view(c)
        cp = pltpu.make_async_copy(ref.at[(*pick(c, 0, False), *tail)], bufs(c)[0], load_sem.at[c])
        loads.append(cp)
    sent = {}
    steps = sorted(((c, s) for c in range(len(chunks)) for s in range(count + 1)), key=lambda cs: (cs[0] + 2 * cs[1], cs[0]))
    for c, s in steps:
        name, lead, lo, size = chunks[c]
        a, l = bufs(c)
        if s > 0:
            sent[c, s - 1].wait_recv()
            if s == 1:
                loads[c].wait()
            r = l[s - 1]
            left = count - s
            if s < count:
                base = pick(c, s - 1, False) if s > 1 else (slice(None),) * (count - 1)

                def add(i, carry, base=base, a=a, r=r, left=left):
                    sub = [lax.rem(i // (1 << (left - 1 - j)), 2) for j in range(left)]
                    it = iter(sub)
                    at = tuple(next(it) if isinstance(b, slice) else b for b in base)
                    a[at] = (a[at].astype(jnp.float32) + r[tuple(sub)].astype(jnp.float32)).astype(a.dtype)
                    return carry

                lax.fori_loop(0, 1 << left, add, 0)
            else:
                at = pick(c, s - 1, False)
                total = a[at].astype(jnp.float32) + r[...].astype(jnp.float32)
                if name == "small":
                    small_o[...] = total
                else:
                    ref = {"qkv": qkv_o, "proj": proj_o, "up": up_o, "down": down_o}[name]
                    if lead is not None:
                        ref = ref.at[lead]
                    ref[:, lo : lo + size] = total
        if s < count:
            if s == 0:
                loads[c].start()
                ref, tail = src_view(c)
                src = ref.at[(*pick(c, 0, True), *tail)]
            else:
                src = a.at[pick(c, s, True)]
            cp = pltpu.make_async_remote_copy(src, l[s], send.at[c * count + s], recv.at[c * count + s],
                                              device_id={"dp": partner_of(me, mine, order_of(c)[s])}, device_id_type=MESH)
            cp.start()
            sent[c, s] = cp
    last = pltpu.make_async_remote_copy(small_o, pair_o, pair_sem.at[0], pair_sem.at[1], device_id={"tensor": other}, device_id_type=MESH)
    last.start()
    for cp in sent.values():
        cp.wait_send()
    last.wait()


def scatter_all(qkv, proj, up, down, small, n, width=512):
    count = n.bit_length() - 1
    two = (2,) * count
    rows = up.shape[-2]
    chunks = [("small", None, 0, 0)]
    for name, a in (("down", down), ("up", up), ("proj", proj)):
        chunks += [(name, None, lo, width) for lo in range(0, a.shape[-1], width)]
    for c in range(3):
        chunks += [("qkv", c, lo, width) for lo in range(0, qkv.shape[-1], width)]
    k = len(chunks)
    f = lambda *s: jax.ShapeDtypeStruct(s, jnp.float32)
    outs = (f(3, rows, qkv.shape[-1]), f(rows, proj.shape[-1]), f(rows, up.shape[-1]), f(rows, down.shape[-1]), f(8, 128), f(8, 128))
    landing = [pltpu.VMEM((k - 1, *two[: count - 1 - s], rows, width), jnp.bfloat16) for s in range(count)]
    landing += [pltpu.VMEM((*two[: count - 1 - s], 8, 128), jnp.float32) for s in range(count)]
    return pl.pallas_call(
        functools.partial(scatter_kernel, count, chunks, width), out_shape=outs,
        in_specs=[ANY] * 5, out_specs=[VM] * 6,
        scratch_shapes=[pltpu.VMEM((k - 1, *two[:-1], rows, width), jnp.bfloat16), pltpu.VMEM((*two[:-1], 8, 128), jnp.float32),
                        pltpu.SemaphoreType.DMA((k,)), pltpu.SemaphoreType.DMA((k * count,)), pltpu.SemaphoreType.DMA((k * count,)),
                        pltpu.SemaphoreType.DMA((2,)), *landing],
        compiler_params=pltpu.CompilerParams(collective_id=1, has_side_effects=True, vmem_limit_bytes=48 * 2**20), name="scatter_all",
    )(qkv, proj, up, down, small)


def swap_kernel(half, src, dst, sems):
    me = lax.axis_index("dp")
    other = 1 - lax.axis_index("tensor")
    barrier = pltpu.get_barrier_semaphore()
    pl.semaphore_signal(barrier, inc=1, device_id={"tensor": other}, device_id_type=MESH)
    pl.semaphore_wait(barrier, 1)
    if half:
        rows = dst.shape[0]
        src = src.at[pl.ds(other * rows, rows)]
    cp = pltpu.make_async_remote_copy(src, dst, sems.at[0], sems.at[1], device_id={"tensor": other}, device_id_type=MESH)
    cp.start()
    cp.wait()


def swap(a, collective_id, half=False):
    shape = (a.shape[0] // 2 if half else a.shape[0], *a.shape[1:])
    return pl.pallas_call(
        functools.partial(swap_kernel, half), out_shape=jax.ShapeDtypeStruct(shape, a.dtype), in_specs=[ANY], out_specs=ANY,
        scratch_shapes=[pltpu.SemaphoreType.DMA((2,))],
        compiler_params=pltpu.CompilerParams(collective_id=collective_id, has_side_effects=True), name="swap%d" % collective_id)(a)


H = 16
HD = 64
SEQ_LEN = 1024
epsilon = 1e-05
gelu_scale = 0.7978845608028654
F32 = jnp.float32
BF = jnp.bfloat16


def gelu_tanh(inputs):
    return 0.5 * inputs * (1.0 + jnp.tanh(gelu_scale * (inputs + 0.044715 * inputs * inputs * inputs)))


def norm_rows(values, gain_row, shift_row):
    center = values - jnp.mean(values, axis=-1, keepdims=True)
    spread = jnp.mean(center * center, axis=-1, keepdims=True)
    inverse = lax.rsqrt(spread + epsilon)
    normed = center * inverse
    return (normed * gain_row + shift_row, normed, inverse)


def norm_back(grad_rows, normed, inverse, gain_row):
    scaled = grad_rows * gain_row
    return inverse * (
        scaled
        - jnp.mean(scaled, axis=-1, keepdims=True)
        - normed * jnp.mean(scaled * normed, axis=-1, keepdims=True)
    )


def contract(left, right, l, r):
    return lax.dot_general(left, right, (((l,), (r,)), ((), ())), preferred_element_type=F32)


def head_slopes(heads_dev):
    head_order = (
        lax.axis_index("tensor") * heads_dev + jnp.arange(heads_dev, dtype=jnp.int32) + 1
    ).astype(F32)
    return 2.0 ** (-8.0 * head_order / H)


def block_scores(queries, keys_all, slopes, q_start):
    block_len = queries.shape[1]
    key_count = keys_all.shape[1]
    scores = jnp.einsum("sqhd,skhd->shqk", queries, keys_all, preferred_element_type=F32) * HD ** (-0.5)
    query_pos = q_start + jnp.arange(block_len, dtype=jnp.int32)
    key_pos = jnp.arange(key_count, dtype=jnp.int32)
    offsets = (key_pos[None, :] - query_pos[:, None]).astype(F32)
    scores = scores + slopes[:, None, None] * offsets
    return jnp.where(key_pos[None, :] <= query_pos[:, None], scores, -1e30)


def attend(queries, keys_all, values_all, slopes):
    block_len = min(512, SEQ_LEN)
    outputs = []
    log_sums = []
    for q_start in range(0, SEQ_LEN, block_len):
        q_end = q_start + block_len
        scores = block_scores(queries[:, q_start:q_end], keys_all[:, :q_end], slopes, q_start)
        row_peak = jnp.max(scores, axis=-1, keepdims=True)
        expweights = jnp.exp(scores - row_peak)
        row_total = jnp.sum(expweights, axis=-1, keepdims=True)
        attn_probs = (expweights / row_total).astype(BF)
        block_out = jnp.einsum("shqk,skhd->sqhd", attn_probs, values_all[:, :q_end], preferred_element_type=F32)
        outputs.append(block_out.astype(BF))
        log_sums.append((row_peak + jnp.log(row_total))[..., 0])
    return (jnp.concatenate(outputs, axis=1), jnp.concatenate(log_sums, axis=2))


def attend_back(queries, keys_all, values_all, grad_out, log_sums, slopes):
    block_len = min(512, SEQ_LEN)
    grad_keys = jnp.zeros(keys_all.shape, F32)
    grad_values = jnp.zeros(values_all.shape, F32)
    grad_queries = []
    for q_start in range(0, SEQ_LEN, block_len):
        q_end = q_start + block_len
        query_part = queries[:, q_start:q_end]
        grad_part = grad_out[:, q_start:q_end]
        scores = block_scores(query_part, keys_all[:, :q_end], slopes, q_start)
        attn_probs = jnp.exp(scores - log_sums[:, :, q_start:q_end, None])
        probs_low = attn_probs.astype(BF)
        grad_probs = jnp.einsum("sqhd,skhd->shqk", grad_part, values_all[:, :q_end], preferred_element_type=F32)
        row_inner = jnp.sum(grad_probs * attn_probs, axis=-1, keepdims=True)
        grad_scores = (attn_probs * (grad_probs - row_inner)).astype(BF)
        grad_queries.append(
            jnp.einsum("shqk,skhd->sqhd", grad_scores, keys_all[:, :q_end], preferred_element_type=F32) * HD ** (-0.5)
        )
        key_term = jnp.einsum("shqk,sqhd->skhd", grad_scores, query_part, preferred_element_type=F32) * HD ** (-0.5)
        grad_keys = grad_keys.at[:, :q_end].add(key_term)
        value_term = jnp.einsum("shqk,sqhd->skhd", probs_low, grad_part, preferred_element_type=F32)
        grad_values = grad_values.at[:, :q_end].add(value_term)
    return (jnp.concatenate(grad_queries, axis=1), grad_keys, grad_values)


def lane_rows(flat, rows):
    gap = rows * 128 - flat.shape[-1]
    return jnp.pad(flat, [(0, 0)] * (flat.ndim - 1) + [(0, gap)]).reshape(*flat.shape[:-1], rows, 128)


def on_device(layer_in, w_qkv, b_qv, w_proj, w_ff1, b_ff1, w_ff2, norm_gains, add_biases, cotangent):
    n = lax.axis_size("dp")
    t = lax.axis_index("tensor")
    two = (2,) * (n.bit_length() - 1)
    local = layer_in.shape[0]
    rows = 2 * local
    seqs = rows // SEQ_LEN
    width = w_qkv.shape[2]
    model = layer_in.shape[1]
    hidden_dev = w_ff1.shape[1]
    heads = b_qv.shape[1]
    part = norm_gains.shape[1]
    mine = lambda a: lax.dynamic_slice_in_dim(a, t * local, local, 0)

    gains_flat = jnp.concatenate([norm_gains, add_biases]).reshape(-1)
    small = jnp.concatenate([
        lane_rows(gains_flat, 2), lane_rows(b_ff1.astype(F32).reshape(-1), 1), lane_rows(b_qv.astype(F32).reshape(-1), 1),
        jnp.zeros((4, 128), F32)])
    qkv_w, proj_w, up_w, down_w, small_all, x_low, cot = gather_all(
        w_qkv, w_proj.T, w_ff1, w_ff2.T, small, layer_in, cotangent, n)
    qkv_w = qkv_w.reshape(3, model, width)
    proj_w = proj_w.reshape(model, width)
    up_w = up_w.reshape(model, hidden_dev)
    down_w = down_w.reshape(model, hidden_dev)
    small_all = small_all.reshape(2, n, 8, 128)
    vectors = small_all[:, :, :2].reshape(2, n, 256)[:, :, : 6 * part].reshape(2, n, 6, part)
    vectors = vectors.transpose(2, 1, 0, 3).reshape(6, model)
    gains, shifts = vectors[:2], vectors[2:]
    here = lax.dynamic_index_in_dim(small_all, t, 0, keepdims=False)
    up_bias = here[:, 2, : b_ff1.size].reshape(n, *b_ff1.shape).transpose(1, 0, 2).reshape(-1)
    qv_bias = here[:, 3, : b_qv.size].reshape(n, *b_qv.shape).transpose(1, 2, 0, 3).reshape(2, width)

    resid = x_low.astype(F32)
    act_one, normed_one, inverse_one = norm_rows(resid, gains[0], shifts[0])
    full_one = act_one.astype(BF)
    mixed = jnp.einsum("rd,cde->cre", full_one, qkv_w, preferred_element_type=F32)
    head_shape = (seqs, SEQ_LEN, heads, HD)
    queries = (mixed[0] + qv_bias[0]).astype(BF).reshape(head_shape)
    keys_all = mixed[1].astype(BF).reshape(head_shape)
    values_all = (mixed[2] + qv_bias[1]).astype(BF).reshape(head_shape)
    slopes = head_slopes(heads)
    attended, log_sums = attend(queries, keys_all, values_all, slopes)
    attn_flat = attended.reshape(rows, width)

    projected = contract(attn_flat, proj_w, 1, 1).astype(BF)
    middle = resid + (projected.astype(F32) + swap(projected, 2).astype(F32)) + shifts[1]
    act_two, normed_two, inverse_two = norm_rows(middle, gains[1], shifts[2])
    full_two = act_two.astype(BF)
    hidden_pre = contract(full_two, up_w, 1, 0) + up_bias
    hidden = gelu_tanh(hidden_pre).astype(BF)
    lowered = contract(hidden, down_w, 1, 1).astype(BF)
    layer_out = (mine(middle) + (mine(lowered).astype(F32) + swap(lowered, 3, True).astype(F32)) + shifts[3]).astype(BF)

    grad_hidden = contract(cot, down_w, 1, 0)
    grad_down = contract(cot, hidden, 0, 0).astype(BF)
    unused_value, gelu_pull = jax.vjp(gelu_tanh, hidden_pre)
    grad_pre = gelu_pull(grad_hidden)[0].astype(BF)
    grad_up_bias = jnp.sum(grad_pre, axis=0, dtype=F32)
    grad_up = contract(full_two, grad_pre, 0, 0).astype(BF)
    back_two = contract(grad_pre, up_w, 1, 1).astype(BF)
    grad_act_two = back_two.astype(F32) + swap(back_two, 4).astype(F32)
    grad_mid = cot.astype(F32) + norm_back(grad_act_two, normed_two, inverse_two, gains[1])
    full_mid = grad_mid.astype(BF)
    grad_attn = contract(full_mid, proj_w, 1, 0).astype(BF).reshape(head_shape)
    grad_proj = contract(full_mid, attn_flat, 0, 0).astype(BF)
    grad_q, grad_k, grad_v = attend_back(queries, keys_all, values_all, grad_attn, log_sums, slopes)
    grad_qkv = [p.reshape(rows, width).astype(BF) for p in (grad_q, grad_k, grad_v)]
    grad_qkv_w = jnp.stack([contract(full_one, p, 0, 0).astype(BF) for p in grad_qkv])
    grad_qv_bias = jnp.stack([jnp.sum(grad_qkv[i], axis=0, dtype=F32) for i in (0, 2)])
    back_one = sum(contract(p, qkv_w[i], 1, 1) for i, p in enumerate(grad_qkv)).astype(BF)
    grad_act_one = mine(back_one).astype(F32) + swap(back_one, 5, True).astype(F32)
    grad_in = mine(grad_mid) + norm_back(grad_act_one, mine(normed_one), mine(inverse_one), gains[0])

    two_rows, mid_rows, cot_rows = mine(grad_act_two), mine(grad_mid), cotangent.astype(F32)
    sums = jnp.stack([
        jnp.sum(grad_act_one * mine(normed_one), axis=0), jnp.sum(two_rows * mine(normed_two), axis=0),
        jnp.sum(grad_act_one, axis=0), jnp.sum(mid_rows, axis=0), jnp.sum(two_rows, axis=0), jnp.sum(cot_rows, axis=0)])
    sums = sums.reshape(6, n, 2, part).transpose(1, 2, 0, 3).reshape(n, 2, 6 * part)
    up_sums = grad_up_bias.reshape(b_ff1.shape[0], n, -1).transpose(1, 0, 2).reshape(n, -1)
    qv_sums = grad_qv_bias.reshape(2, heads, n, -1).transpose(2, 0, 1, 3).reshape(n, -1)
    packed = jnp.concatenate([
        lane_rows(sums, 2).reshape(n, 4, 128), lane_rows(up_sums, 1), lane_rows(qv_sums, 1), jnp.zeros((n, 2, 128), F32)], axis=1)
    blocks = lambda a, lead=(): a.reshape(*lead, *two, model // n, a.shape[-1])
    out_qkv, out_proj, out_up, out_down, own, pair = scatter_all(
        blocks(grad_qkv_w, (3,)), blocks(grad_proj), blocks(grad_up), blocks(grad_down), packed.reshape(*two, 8, 128), n)
    both = lax.dynamic_slice_in_dim(own + pair, 2 * t, 2, 0).reshape(-1)[: 6 * part].reshape(6, part)
    return (
        layer_out,
        grad_in,
        out_qkv,
        own[5, : b_qv.size].reshape(b_qv.shape),
        out_proj.T,
        out_up,
        own[4, : b_ff1.size].reshape(b_ff1.shape),
        out_down.T,
        both[:2],
        both[2:],
    )


def solution(mesh):
    rows, cols = P(("dp", "tensor"), None), P(None, ("dp", "tensor"))
    return jax.shard_map(
        on_device,
        mesh=mesh,
        in_specs=(rows, P(None, "dp", "tensor"), P(None, "tensor", "dp"), P("tensor", "dp"), P("dp", "tensor"),
                  P("tensor", "dp"), P("tensor", "dp"), cols, cols, rows),
        out_specs=(rows, rows, P(None, "dp", "tensor"), P(None, "tensor", "dp"), P("tensor", "dp"), P("dp", "tensor"),
                   P("tensor", "dp"), P("tensor", "dp"), cols, cols),
        check_vma=False,
    )
```

time: 1550 us -> 490 us (0.32)
  waiting for transfers between devices: 1060 us -> 0 us
  Pallas kernels: 0 us -> 264 us
  blocking collectives: 238 us -> 0 us
  matrix products: 145 us -> 124 us
    reduce_scatter x7 -> x0, waiting for transfers between devices: 468 us -> none  [the longest x1 183 us: on_device(): lax.psum_scatter(grad_up, 'dp', scatter_dimension=0, tiled=True)]
    unnamed x21 -> x0, waiting for transfers between devices: 394 us -> none
    pallas_call x0 -> x6, Pallas kernels: none -> 264 us  [the longest x1 125 us: gather_all(): pl.pallas_call(functools.partial(gather_kernel, count, chunks), out_shape...]
    all_gather x8 -> x0, waiting for transfers between devices: 197 us -> none  [the longest x1 79.6 us: fetch_mlp(): lax.all_gather(w_ff2, 'dp', axis=1, tiled=True)]
    all_gather x4 -> x0, blocking collectives: 160 us -> none  [the longest x1 43.6 us: on_device(): lax.all_gather(norm_gains, ('dp', 'tensor'), axis=1, tiled=True)]
    unnamed x1 -> x0, blocking collectives: 78.1 us -> none
    dot_general x14 -> x18, matrix products: 104 us -> 80.6 us  [the longest x15 68 us: contract(): lax.dot_general(left, right, (((l,), (r,)), ((), ())), preferred_element_...]
  transfers between devices with their start and end apart: 18 -> 0, of which waited for: 16 -> 0; matrix products, arithmetic and copies ran while one was open for 7% -> 0% of each run, Pallas kernels for 0% -> 0%
where the time goes in v1:
time: 490 us; the launch traced here: 481 us
  Pallas kernels  264 us (54%)
  matrix products  124 us (25%)
  other arithmetic  51.9 us (11%)
  local copies, waits for them, and re-layouts  38.4 us (8%)
    pallas_call x1, Pallas kernels, gather_all(): pl.pallas_call(functools.partial(gather_kernel, count, chunks), out_shape...  125 us
    pallas_call x1, Pallas kernels, scatter_all(): pl.pallas_call(functools.partial(scatter_kernel, count, chunks, width), o...  124 us
    dot_general x15, matrix products, contract(): lax.dot_general(left, right, (((l,), (r,)), ((), ())), preferred_element_...  68 us
    unnamed x123, local copies, waits for them, and re-layouts  25.8 us
    dot_general x2, matrix products, attend_back(): jnp.einsum('sqhd,skhd->shqk', grad_part, values_all[:, :q_end], preferred...  16.2 us
    pallas_call x4, Pallas kernels, swap(): pl.pallas_call(functools.partial(swap_kernel, half), out_shape=jax.ShapeD...  15.1 us
    convert_element_type x2, other arithmetic, attend_back(): grad_scores = (attn_probs * (grad_probs - row_inner)).astype(BF)  14.6 us
    dot_general x2, matrix products, attend_back(): jnp.einsum('shqk,sqhd->skhd', probs_low, grad_part, preferred_element_typ...  13.5 us

profile of v1, /device:TPU:0, one launch (start us, length us, event | category | flops | bytes accessed | tf_op | source)
XLA Modules:
  0.0 480.6 jit_solution(5041367782508386781)
XLA Ops:
  10.5 124.8 %gather_all.1 = (bf16[3,2,2,2,2,64,512]{6,5,4,3,2,1,0:T(8,128)(2,1)}, bf16[2,2,2,2,64,512]{5,4,3,2,1,0:T(8,128)(2,1)}, bf16[2,2,2,2,64,2048]{5,4,3,2,1,0:T(8,128...) custom-call(bf16[3,64,512]{2,1,0:T(8,128)(2,1)} %qkv.1, ...), custom_call_target="tpu_custom_call" | custom-call | tf_op jit(solution)/shard_map/gather_all/pallas_call | solution.py:115
  142.8 3.8 fusion.58
  146.6 3.9 convolution_bitcast_fusion
  160.7 6.3 %fusion.61 = (f32[8,512]{1,0:T(8,128)S(1)}, f32[8,512,1024]{2,1,0:T(8,128)S(1)}) fusion(f32[512,1024]{1,0:T(8,128)} %subtract_convert_fusion, f32[8]{0:T(128)S(1)} %multiply_power_fusion, bf16[1024,8,64]{0,2,1:T(8,128)(2,1)S(1)} %bitcast.172, bf16[1,1024,8,64]{1,3,2,0:T(8,128)(2,1)} %copy-done.21, pred[512,1024]{1,0:T(8,128)(4,1)} %iota_compare_fusion), kind=kOutput, calls=%fused_computation.152 | convolution fusion | flops 557838336 | bytes 20987936 | tf_op jit(solution)/shard_map/sqhd,skhd->shqk/dot_general | solution.py:311
  167.1 3.8 fusion
  172.8 4.4 fusion.38
  178.4 3.8 convolution_convert_fusion.4.src
  182.2 4.5 swap2.1
  186.8 4.7 fusion.55
  197.1 4.5 fusion.47
  201.6 7.0 %convolution_convert_fusion.3.src = bf16[1024,1024]{1,0:T(8,128)(2,1)} fusion(bf16[1024,2048]{1,0:T(8,128)(2,1)S(1)} %bitcast.218, f32[1024,2048]{1,0:T(8,128)S(1)} %fusion.47, f32[2048]{0:T(1024)S(1)} %add.294), kind=kOutput, calls=%fused_computation.77 | convolution fusion | flops 4316987392 | bytes 14688256 | tf_op jit(solution)/shard_map/dot_general | solution.py:298
  208.6 12.3 %convert_reduce_fusion = (f32[2048]{0:T(1024)S(1)}, bf16[1024,2048]{1,0:T(8,128)(2,1)}) fusion(f32[1024,2048]{1,0:T(8,128)S(1)} %fusion.47, f32[2048]{0:T(1024)S(1)} %add.294, bf16[1024,1024]{1,0:T(8,128)(2,1)S(1)} %copy-done.27, bf16[1024,2048]{1,0:T(8,128)(2,1)S(1)} %bitcast.219), kind=kOutput, calls=%fused_computation.19 | convolution fusion | flops 4351588352 | bytes 18890752 | tf_op jit(solution)/shard_map/dot_general | solution.py:298
  220.9 6.5 %convolution_convert_fusion = bf16[1024,2048]{1,0:T(8,128)(2,1)} fusion(bf16[1024,1024]{1,0:T(8,128)(2,1)S(1)} %copy-done.27, f32[1024,2048]{1,0:T(8,128)S(1)} %fusion.47, f32[2048]{0:T(1024)S(1)} %add.294), kind=kOutput, calls=%fused_computation.49 | convolution fusion | flops 4318035968 | bytes 14688256 | tf_op jit(solution)/shard_map/dot_general | solution.py:298
  227.4 5.9 %convolution_convert_fusion.2.src = bf16[1024,1024]{1,0:T(8,128)(2,1)} fusion(bf16[1024,2048]{1,0:T(8,128)(2,1)S(1)} %copy-done.51, bf16[1024,2048]{1,0:T(8,128)(2,1)S(1)} %bitcast.217), kind=kOutput, calls=%fused_computation.76 | convolution fusion | flops 4296015872 | bytes 10485760 | tf_op jit(solution)/shard_map/dot_general | solution.py:298
  236.9 4.5 swap4.1
  241.5 10.1 %convolution_convert_fusion.1 = bf16[1024,2048]{1,0:T(8,128)(2,1)} fusion(bf16[1024,2048]{1,0:T(8,128)(2,1)} %get-tuple-element.149, f32[1024,1024]{1,0:T(8,128)} %copy-done.17, f32[1024]{0:T(1024)S(1)} %add.291, f32[1024]{0:T(1024)S(1)} %mul.295), kind=kOutput, calls=%fused_computation.50 | convolution fusion | flops 4300210176 | bytes 12591104 | tf_op jit(solution)/shard_map/dot_general | solution.py:298
  261.9 4.8 fusion.30
  266.7 8.7 %convert_reduce_fusion.2 = (f32[8,64]{1,0:T(8,128)S(1)}, bf16[1,1024,8,64]{1,3,2,0:T(8,128)(2,1)}) fusion(f32[8,512,1024]{2,1,0:T(8,128)} %copy-done.4, f32[8,512]{1,0:T(8,128)S(1)} %log_add_fusion, bf16[1,1024,8,64]{1,3,2,0:T(8,128)(2,1)S(1)} %bitcast.176, f32[1,512,8,64]{1,3,2,0:T(8,128)S(1)} %fusion.30), kind=kOutput, calls=%fused_computation.61 | convolution fusion | flops 547356160 | bytes 19417088 | tf_op jit(solution)/shard_map/shqk,sqhd->skhd/dot_general | solution.py:356
  275.6 4.0 convolution_convert_fusion.6
  279.6 5.1 %multiply_reduce_fusion.1 = (f32[8,512]{1,0:T(8,128)S(1)}, f32[8,512,512]{1,2,0:T(8,128)S(1)}) fusion(f32[8,512,512]{1,2,0:T(8,128)} %copy-done.5, f32[8,512]{1,0:T(8,128)S(1)} %log_add_fusion.1, f32[1,1024,8,64]{1,3,2,0:T(8,128)S(1)} %bitcast.168, f32[8,64]{1,0:T(8,128)S(1)} %copy.94, bf16[1,1024,8,64]{1,3,2,0:T(8,128)(2,1)S(1)} %bitcast.177), kind=kOutput, calls=%fused_computation.22 | convolution fusion | flops 275247104 | bytes 18386944 | tf_op jit(solution)/shard_map/sqhd,skhd->shqk/dot_general | solution.py:348
  290.7 11.1 %multiply_reduce_fusion = (f32[8,512]{1,0:T(8,128)S(1)}, f32[8,512,1024]{2,1,0:T(8,128)}) fusion(f32[8,512,1024]{2,1,0:T(8,128)} %copy-done.4, f32[8,512]{1,0:T(8,128)S(1)} %log_add_fusion, f32[1024,8,64]{0,2,1:T(8,128)S(1)} %bitcast.169, f32[8,64]{1,0:T(8,128)S(1)} %copy.94, bf16[1,1024,8,64]{1,3,2,0:T(8,128)(2,1)S(1)} %bitcast.178), kind=kOutput, calls=%fused_computation.1 | convolution fusion | flops 550498304 | bytes 36212736 | tf_op jit(solution)/shard_map/sqhd,skhd->shqk/dot_general | solution.py:348
  301.8 12.0 %multiply_convert_fusion = bf16[8,512,1024]{2,1,0:T(8,128)(2,1)S(1)} fusion(f32[8,512,1024]{2,1,0:T(8,128)} %get-tuple-element.176, f32[8,512,1024]{2,1,0:T(8,128)} %copy-done.4, f32[8,512]{1,0:T(8,128)S(1)} %get-tuple-element.175, f32[8,512]{1,0:T(8,128)S(1)} %log_add_fusion), kind=kLoop, calls=%fused_computation | loop fusion | flops 16777216 | bytes 41975808 | tf_op jit(solution)/shard_map/convert_element_type | solution.py:350
  332.7 6.2 %multiply_reduce_fusion.6 = (f32[1024]{0:T(1024)S(1)}, f32[512]{0:T(512)S(1)}, f32[512]{0:T(512)S(1)}, f32[1024]{0:T(1024)S(1)}, bf16[512,1024]{1,0:T(8,128)(2,1)}) fusion(bf16[512,1024]{1,0:T(8,128)(2,1)} %swap5.1, f32[1024,1024]{1,0:T(8,128)} %get-tuple-element.162, s32[]{:T(128)S(6)} %select_n.34, bf16[1024,1024]{1,0:T(8,128)(2,1)} %add_convert_fusion.src, ...), kind=kLoop, calls=%fused_computation.65 | loop fusion | flops 8385536 | bytes 9457668 | tf_op jit(solution)/shard_map/reduce_sum | solution.py:441
  344.5 124.5 %scatter_all.1 = (f32[3,64,512]{2,1,0:T(8,128)S(1)}, f32[64,512]{1,0:T(8,128)S(1)}, f32[64,2048]{1,0:T(8,128)S(1)}, f32[64,2048]{1,0:T(8,128)S(1)}, f32[8,128]{1,0:T(8,128)S(1)}, /*index=5*/f32[8,128]{1,0:T(8,128)S(1)}) custom-call(bf16[3,2,2,2,2,64,512]{6,5,4,3,2,1,0:T(8,128)(2,1)S(1)} %pad_maximum_fusion.qkv, ...), custom_call_target="tpu_custom_call" | custom-call | tf_op jit(solution)/shard_map/scatter_all/pallas_call | solution.py:235
  (239 shorter events, 91.1 us)
Async XLA Ops:
  135.4 4.9 %copy-start.39 = (f32[2,2,2,2,2,8,128]{6,5,4,3,2,1,0:T(8,128)S(1)}, f32[2,2,2,2,2,8,128]{6,5,4,3,2,1,0:T(8,128)}, u32[]{:S(2)}) copy-start(f32[2,2,2,2,2,8,128]{6,5,4,3,2,1,0:T(8,128)} %get-tuple-element.89) | copy-start | bytes 393220
  140.5 6.1 %copy-start.11 = (bf16[1024,1024]{1,0:T(8,128)(2,1)S(1)}, bf16[1024,1024]{1,0:T(8,128)(2,1)}, u32[]{:S(2)}) copy-start(bf16[1024,1024]{1,0:T(8,128)(2,1)} %get-tuple-element.87) | copy-start | bytes 6291460
  141.7 4.9 %copy-start.45 = (f32[1024]{0:T(1024)}, f32[1024]{0:T(1024)S(1)}, u32[]{:S(2)}) copy-start(f32[1024]{0:T(1024)S(1)} %add.266) | copy-start | bytes 12292
  141.8 4.8 %copy-start.41 = (f32[1024]{0:T(1024)}, f32[1024]{0:T(1024)S(1)}, u32[]{:S(2)}) copy-start(f32[1024]{0:T(1024)S(1)} %mul.279) | copy-start | bytes 12292
  150.6 10.1 %copy-start.19 = (bf16[1,1024,512]{1,2,0:T(8,128)(2,1)}, bf16[1,1024,512]{1,2,0:T(8,128)(2,1)S(1)}, u32[]{:S(2)}) copy-start(bf16[1,1024,512]{1,2,0:T(8,128)(2,1)S(1)} %slice.298) | copy-start | bytes 3145732
  151.2 19.7 %copy-start.13 = (f32[1,1024,512]{1,2,0:T(8,128)}, f32[1,1024,512]{1,2,0:T(8,128)S(1)}, u32[]{:S(2)}) copy-start(f32[1,1024,512]{1,2,0:T(8,128)S(1)} %get-tuple-element.154) | copy-start | bytes 6291460
  167.1 5.7 %copy-start.4 = (f32[8,512,1024]{2,1,0:T(8,128)}, f32[8,512,1024]{2,1,0:T(8,128)S(1)}, u32[]{:S(2)}) copy-start(f32[8,512,1024]{2,1,0:T(8,128)S(1)} %get-tuple-element.172) | copy-start | bytes 50331652
  172.8 4.4 copy-start.38
  197.1 4.5 copy-start.49
  201.6 7.0 %copy-start.27 = (bf16[1024,1024]{1,0:T(8,128)(2,1)S(1)}, bf16[1024,1024]{1,0:T(8,128)(2,1)}, u32[]{:S(2)}) copy-start(bf16[1024,1024]{1,0:T(8,128)(2,1)} %get-tuple-element.93) | copy-start | bytes 6291460
  220.9 6.5 %copy-start.51 = (bf16[1024,2048]{1,0:T(8,128)(2,1)S(1)}, bf16[1024,2048]{1,0:T(8,128)(2,1)}, u32[]{:S(2)}) copy-start(bf16[1024,2048]{1,0:T(8,128)(2,1)} %get-tuple-element.149) | copy-start | bytes 12582916
  241.4 10.2 %copy-start.7 = (f32[1024,1024]{1,0:T(8,128)S(1)}, f32[1024,1024]{1,0:T(8,128)}, u32[]{:S(2)}) copy-start(f32[1024,1024]{1,0:T(8,128)} %copy-done.6) | copy-start | bytes 12582916
  241.4 10.2 %copy-start.8 = (bf16[1024,1024]{1,0:T(8,128)(2,1)S(1)}, bf16[1024,1024]{1,0:T(8,128)(2,1)}, u32[]{:S(2)}) copy-start(bf16[1024,1024]{1,0:T(8,128)(2,1)} %convolution_convert_fusion.2.src) | copy-start | bytes 6291460
  241.4 10.1 %copy-start.10 = (bf16[1024,1024]{1,0:T(8,128)(2,1)S(1)}, bf16[1024,1024]{1,0:T(8,128)(2,1)}, u32[]{:S(2)}) copy-start(bf16[1024,1024]{1,0:T(8,128)(2,1)} %swap4.1) | copy-start | bytes 6291460
  266.7 8.8 %copy-start.42 = (f32[1024]{0:T(1024)S(1)}, f32[1024]{0:T(1024)}, u32[]{:S(2)}) copy-start(f32[1024]{0:T(1024)} %copy-done.41) | copy-start | bytes 12292
  266.7 8.8 %copy-start.46 = (f32[1024]{0:T(1024)S(1)}, f32[1024]{0:T(1024)}, u32[]{:S(2)}) copy-start(f32[1024]{0:T(1024)} %copy-done.45) | copy-start | bytes 12292
  279.6 5.1 %slice-start = ((s8[8388608]{0:T(1024)(128)(4,1)}), s8[4194304]{0:T(1024)(128)(4,1)S(1)}, s32[]{:S(2)}) async-start(s8[8388608]{0:T(1024)(128)(4,1)} %bitcast.164), calls=%async_computation | async-start | bytes 8388608
  279.6 5.9 %slice-start.1 = ((s8[8388608]{0:T(1024)(128)(4,1)}), s8[4194304]{0:T(1024)(128)(4,1)S(1)}, s32[]{:S(2)}) async-start(s8[8388608]{0:T(1024)(128)(4,1)} %bitcast.164), calls=%async_computation.1 | async-start | bytes 8388608
  289.3 30.6 %copy-start.29 = (bf16[1,512,8,64]{1,3,2,0:T(8,128)(2,1)}, bf16[1,512,8,64]{1,3,2,0:T(8,128)(2,1)S(1)}, u32[]{:S(2)}) copy-start(bf16[1,512,8,64]{1,3,2,0:T(8,128)(2,1)S(1)} %fusion.34) | copy-start | bytes 1572868
  327.0 5.7 %copy-start.43 = (f32[1024]{0:T(1024)S(1)}, f32[1024]{0:T(1024)}, u32[]{:S(2)}) copy-start(f32[1024]{0:T(1024)} %add.301) | copy-start | bytes 12292
  332.7 6.3 %copy-start.9 = (bf16[1024,1024]{1,0:T(8,128)(2,1)S(1)}, bf16[1024,1024]{1,0:T(8,128)(2,1)}, u32[]{:S(2)}) copy-start(bf16[1024,1024]{1,0:T(8,128)(2,1)} %add_convert_fusion.src) | copy-start | bytes 6291460
  332.7 6.2 %copy-start.12 = (f32[1024,1024]{1,0:T(8,128)S(1)}, f32[1024,1024]{1,0:T(8,128)}, u32[]{:S(2)}) copy-start(f32[1024,1024]{1,0:T(8,128)} %get-tuple-element.162) | copy-start | bytes 12582916
  332.7 6.2 %copy-start.16 = (bf16[512,1024]{1,0:T(8,128)(2,1)S(1)}, bf16[512,1024]{1,0:T(8,128)(2,1)}, u32[]{:S(2)}) copy-start(bf16[512,1024]{1,0:T(8,128)(2,1)} %swap5.1) | copy-start | bytes 3145732
  332.7 6.2 %copy-start.44 = (f32[512]{0:T(512)S(1)}, f32[512]{0:T(512)}, u32[]{:S(2)}) copy-start(f32[512]{0:T(512)} %dynamic-slice.29) | copy-start | bytes 6148
  (30 other events, 70.0 us)
